TPU v7x, 32 devices: a whole 2x2x4 slice. The times are simulated.
32 devices in a mesh: row: 8 (over y, x, core), col: 4 (over z).
Axes of the slice: x: 2, y: 2, z: 4, core: 2. Of those that a mesh axis runs over, the one named last changes fastest.
Arguments:
- p_cov: bfloat16 [4096, 4096], P('row', 'col'), may hold values from -6 to 6, as said below
- f_blocks: bfloat16 [32, 7, 128, 128], P('row'), may hold values from -0.1875 to 0.1875
- stencil_cols: int32 [32, 7], replicated, may hold values from 0 to 31, as said below
- localization_weights: bfloat16 [4096, 4096], P('row', 'col'), may hold values from 0.25 to 1, as said below
- block_mask: int32 [32, 32], P('row', 'col'), may hold values from 0 to 1, as said below
- disturbance_variances: float32 [4096], P('row'), may hold values from 0.5 to 2
Outputs:
- predicted_spread_matrix: float32 [4096, 4096], P('row', 'col')
Inputs may be any that keep to these rules, and one draw needn't show every extreme that they name: `stencil_cols`: block row i lists i, i - 1, i + 1, one block 2 to 3 above and one below, and i - 4 and i + 4, each clamped to 0 .. 31. Symmetric: p_cov equals its transpose. `localization_weights`: Symmetric: taper equals its transpose. Symmetric: block_mask equals its transpose.
All inputs are finite; a program needn't handle non-finite values.
Results may differ from a plain program's by a relative error of at most 0.0029.
Values may be sent and summed in bfloat16 or wider, within the bound.
No kernel may reach another device: no remote copies, remote signals or barrier semaphores. Data moves between devices by JAX's collectives and lax.ppermute only.
A program may use at most 64 MiB of HBM per device.

v0:
```python
import functools

import jax
import jax.numpy as jnp
from jax import lax
from jax.experimental import pallas as pl
from jax.experimental.pallas import tpu as pltpu
from jax.sharding import PartitionSpec as P


STENCIL = 7
BAND = 4
ANY = pl.ANY


def exchanges(devices):
    both = []
    for start in (0, 1):
        pairs = [(i, i + 1) for i in range(start, devices - 1, 2)]
        both.append(pairs + [(j, i) for i, j in pairs])
    return both


def source_plane(c, a, cols):
    if cols & (cols - 1):
        return a
    return c ^ (((a ^ c) - 1) % cols)


def group_plan(rows, cols):
    fan = rows // cols

    def at(a, k, c):
        return (a * fan + k) * cols + c

    if (cols, fan) != (4, 2):
        pairs = []
        for c in range(cols):
            for a in range(cols):
                if a != c:
                    plane = source_plane(c, a, cols)
                    pairs += [(at(c, k, plane), at(a, k, c)) for k in range(fan)]
        return [(0, pairs)]
    first, relayed, second = [], [], []
    for c in range(cols):
        near, side, far = c ^ 1, c ^ 2, c ^ 3
        i, j = (1, 0) if c in (1, 2) else (0, 1)
        first += [(at(c, i, c), at(near, i, c)), (at(c, j, c), at(side, j, c))]
        relayed += [(at(near, i, c), at(far, i, c)), (at(side, j, c), at(far, j, c))]
        second += [(at(c, i, c), at(side, i, c)), (at(c, j, c), at(near, j, c))]
    return [(0, first), (1, relayed), (0, second)]


def holder_table(rows, cols):
    table = [0] * (rows * cols)
    for step, (_, pairs) in enumerate(group_plan(rows, cols)):
        for _, target in pairs:
            table[target] = step + 1
    return table


def pick_kernel(table, *refs):
    *sources, out_ref, sem = refs
    me = lax.axis_index("row") * lax.axis_size("col") + lax.axis_index("col")
    which = 0
    for device, step in enumerate(table):
        if step:
            which = jnp.where(me == device, step, which)
    for step, source in enumerate(sources):

        @pl.when(which == step)
        def _():
            copies = [
                pltpu.make_async_copy(source.at[n], out_ref.at[n], sem.at[n])
                for n in range(out_ref.shape[0])
            ]
            for copy in copies:
                copy.start()
            for copy in copies:
                copy.wait()


def fetch_kernel(f_hbm, cols_hbm, f_ref, cols_ref, sem):
    copies = [
        pltpu.make_async_copy(f_hbm, f_ref, sem.at[0]),
        pltpu.make_async_copy(cols_hbm, cols_ref, sem.at[1]),
    ]
    for copy in copies:
        copy.start()
    for copy in copies:
        copy.wait()


def stage1_kernel(bent, cols_ref, f_ref, top_hbm, bottom_hbm, inner_hbm, outer_hbm, *refs):
    *halves, first_ref, second_ref, ext, sem = refs
    rows, bs = f_ref.shape[0], f_ref.shape[2]
    half = first_ref.shape[1]
    row_idx, col_idx = lax.axis_index("row"), lax.axis_index("col")
    base = row_idx * rows
    halo, part = inner_hbm.shape[0], top_hbm.shape[0]
    below = halo + 2 * part
    odd = lax.rem(row_idx, 2)
    inner_at = pl.multiple_of((1 - odd) * below, bs)
    outer_at = pl.multiple_of(odd * below, bs)

    def copies(at, pieces, sems):
        for piece, n in zip(pieces, sems):
            yield pltpu.make_async_copy(piece, ext.at[pl.ds(at, piece.shape[0])], sem.at[n])
            at += piece.shape[0]

    def all_copies(act):
        for copy in copies(halo, (top_hbm, bottom_hbm), (0, 1)):
            act(copy)
        for copy in copies(inner_at, (inner_hbm,), (2,)):
            act(copy)
        if not halves:
            for copy in copies(outer_at, (outer_hbm,), (3,)):
                act(copy)
            return
        is_bent = (row_idx == bent[0]) | (row_idx == bent[1])

        @pl.when(jnp.logical_not(is_bent))
        def _():
            for copy in copies(outer_at, (outer_hbm,), (3,)):
                act(copy)

        @pl.when(is_bent)
        def _():
            for copy in copies(outer_at, halves, (3, 4)):
                act(copy)

    all_copies(lambda copy: copy.start())
    all_copies(lambda copy: copy.wait())
    tile = min(256, half)
    odd = lax.rem(col_idx, 2)
    for i in range(rows):
        lhs = jnp.concatenate([f_ref[i, e] for e in range(STENCIL)], axis=1)
        starts = [
            pl.multiple_of((cols_ref[e, base + i] - base + BAND) * bs, bs)
            for e in range(STENCIL)
        ]
        for part, out_ref in ((1 - odd, first_ref), (odd, second_ref)):
            for t in range(half // tile):
                at = pl.ds(pl.multiple_of(part * half + t * tile, bs), tile)
                rhs = jnp.concatenate([ext[pl.ds(s, bs), at] for s in starts], axis=0)
                out_ref[i * bs : (i + 1) * bs, t * tile : (t + 1) * tile] = jnp.dot(
                    lhs, rhs, preferred_element_type=jnp.float32
                ).astype(out_ref.dtype)


def stage2_kernel(fan, turn, cols_ref, mask_ref, q_ref, w_ref, f_ref, *refs):
    ready = []
    if turn == 0:
        *parts, made, ext, sem = refs
    else:
        ext, *ready = refs[:-4] if turn == fan - 1 else refs[:-1]
        parts = []
        if turn == fan - 1:
            out_hbm, made, out_sem, ready_sem = refs[-4:]
        else:
            made = refs[-1]
    group, bs = f_ref.shape[0], f_ref.shape[2]
    rows, slab = mask_ref.shape
    row_idx, col_idx = lax.axis_index("row"), lax.axis_index("col")
    first = col_idx * slab - BAND

    def column(turn, n):
        return lax.rem(row_idx + turn, fan) * group + n

    def place(j):
        return pl.ds(pl.multiple_of(j * bs, bs), bs)

    stores = []
    for before, done in enumerate(ready):
        for n in range(group):
            to = out_hbm.at[:, place(column(before, n))]
            stores.append(pltpu.make_async_copy(done.at[n], to, ready_sem.at[before, n]))
    joins = []
    odd = lax.rem(col_idx, 2)
    for piece, part in enumerate(parts):
        width = part.shape[1]
        at = odd * piece + (1 - odd) * (len(parts) - 1 - piece)
        to = ext.at[:, pl.ds(pl.multiple_of(at * width, width), width)]
        joins.append(pltpu.make_async_copy(part, to, sem.at[piece]))
    for copy in joins + stores:
        copy.start()
    for copy in joins:
        copy.wait()

    eye = lax.broadcasted_iota(jnp.int32, (bs, bs), 0) == lax.broadcasted_iota(
        jnp.int32, (bs, bs), 1
    )
    for n in range(group):
        j = column(turn, n)
        col = col_idx * slab + j
        to = place(j)
        lhs = jnp.concatenate(
            [
                ext[:, pl.ds(pl.multiple_of((cols_ref[e, col] - first) * bs, bs), bs)]
                for e in range(STENCIL)
            ],
            axis=1,
        )
        rhs = jnp.concatenate([f_ref[n, e] for e in range(STENCIL)], axis=1)
        spread = lax.dot_general(
            lhs, rhs, (((1,), (1,)), ((), ())), preferred_element_type=jnp.float32
        )
        for i in range(rows):
            at = slice(i * bs, (i + 1) * bs)
            keep = mask_ref[i, j].astype(jnp.float32)
            on_main = (row_idx * rows + i == col).astype(jnp.float32)
            noise = jnp.where(eye, q_ref[i : i + 1, :] * on_main, 0.0)
            made[n, at, :] = w_ref[at, to].astype(jnp.float32) * (spread[at] * keep) + noise
        if turn == fan - 1:
            store = pltpu.make_async_copy(made.at[n], out_hbm.at[:, to], out_sem.at[n])
            store.start()
            stores.append(store)
    for store in stores:
        store.wait()


def forecast(
    p_cov, f_blocks, stencil_cols, localization_weights, block_mask, disturbance_variances
):
    rows, cols = lax.axis_size("row"), lax.axis_size("col")
    fan = rows // cols
    block_rows, bs = f_blocks.shape[0], f_blocks.shape[2]
    tall, wide = p_cov.shape
    slab = wide // bs
    halo = BAND * bs
    assert tall == halo and wide == 2 * halo
    cols_of = stencil_cols.T

    smem = pl.BlockSpec(memory_space=pltpu.SMEM)
    hbm = pl.BlockSpec(memory_space=ANY)
    vmem = pl.BlockSpec(memory_space=pltpu.VMEM)
    top, bottom = p_cov[: tall // 2], p_cov[tall // 2 :]
    f_near, cols_of = pl.pallas_call(
        fetch_kernel,
        out_shape=tuple(jax.ShapeDtypeStruct(x.shape, x.dtype) for x in (f_blocks, cols_of)),
        in_specs=[hbm, hbm],
        out_specs=(vmem, vmem),
        scratch_shapes=[pltpu.SemaphoreType.DMA((2,))],
        compiler_params=pltpu.CompilerParams(vmem_limit_bytes=8 * 2**20),
        name="fetch",
    )(f_blocks, cols_of)

    inner_pairs, outer_pairs = exchanges(rows)
    bent, halves = (rows // 2, rows // 2 - 1), ()
    if (cols, fan) == (4, 2):
        lower, upper = bent
        across = [(upper, lower), (lower, upper)]
        outer_pairs = [pair for pair in outer_pairs if pair not in across]
        straight = lax.ppermute(top, "row", across)
        turn = lax.ppermute(bottom, "row", [(upper, rows - 1), (lower, 0)])
        turned = lax.ppermute(turn, "row", [(rows - 1, lower), (0, upper)])
        halves = (straight, turned)
    inner = lax.ppermute(p_cov, "row", inner_pairs)
    outer = lax.ppermute(p_cov, "row", outer_pairs)
    held = [f_blocks]
    for source, pairs in group_plan(rows, cols):
        held.append(lax.ppermute(held[source], ("row", "col"), pairs))

    half = jax.ShapeDtypeStruct((tall, halo), jnp.bfloat16)
    first, second = pl.pallas_call(
        functools.partial(stage1_kernel, bent),
        out_shape=(half, half),
        in_specs=[smem, vmem] + [hbm] * (4 + len(halves)),
        out_specs=(vmem, vmem),
        scratch_shapes=[
            pltpu.VMEM((tall + 2 * halo, wide), jnp.bfloat16),
            pltpu.SemaphoreType.DMA((5,)),
        ],
        compiler_params=pltpu.CompilerParams(vmem_limit_bytes=16 * 2**20),
        name="stage1",
    )(cols_of, f_near, top, bottom, inner, outer, *halves)

    inner_pairs, outer_pairs = exchanges(cols)
    idle = set(range(cols)) - {i for i, _ in outer_pairs}
    outer_pairs = outer_pairs + [(i, i) for i in sorted(idle)]
    nearer = lax.ppermute(first, "col", inner_pairs)
    further = lax.ppermute(second, "col", outer_pairs)

    mine = pl.pallas_call(
        functools.partial(pick_kernel, holder_table(rows, cols)),
        out_shape=jax.ShapeDtypeStruct(f_blocks.shape, f_blocks.dtype),
        in_specs=[vmem] * len(held),
        out_specs=vmem,
        scratch_shapes=[pltpu.SemaphoreType.DMA((block_rows,))],
        compiler_params=pltpu.CompilerParams(vmem_limit_bytes=4 * 2**20),
        name="pick",
    )(*held)
    fixed = (
        cols_of,
        block_mask,
        disturbance_variances.reshape(block_rows, bs),
        localization_weights,
    )
    assert fan > 1
    group = slab // fan
    made_type = jax.ShapeDtypeStruct((group, tall, bs), jnp.float32)
    params = pltpu.CompilerParams(vmem_limit_bytes=20 * 2**20)
    made, ext = pl.pallas_call(
        functools.partial(stage2_kernel, fan, 0),
        out_shape=(made_type, jax.ShapeDtypeStruct((tall, wide + 2 * halo), jnp.bfloat16)),
        in_specs=[smem, smem, vmem, vmem, vmem] + [hbm] * 4,
        out_specs=(vmem, vmem),
        scratch_shapes=[pltpu.SemaphoreType.DMA((4,))],
        compiler_params=params,
        name="stage2",
    )(*fixed, mine, nearer, first, second, further)
    ready = [made]
    for turn in range(1, fan):
        last = turn == fan - 1
        pairs = [(r // fan * fan + (r + turn) % fan, r) for r in range(rows)]
        other = lax.ppermute(mine, "row", pairs)
        ready.append(
            pl.pallas_call(
                functools.partial(stage2_kernel, fan, turn),
                out_shape=jax.ShapeDtypeStruct((tall, wide), jnp.float32) if last else made_type,
                in_specs=[smem, smem, vmem, vmem, vmem, vmem] + [vmem] * (len(ready) * last),
                out_specs=pl.BlockSpec(memory_space=pltpu.HBM) if last else vmem,
                scratch_shapes=[
                    pltpu.VMEM(made_type.shape, made_type.dtype),
                    pltpu.SemaphoreType.DMA((group,)),
                    pltpu.SemaphoreType.DMA((turn, group)),
                ]
                * last,
                compiler_params=params,
                name="stage3",
            )(*fixed, other, ext, *(ready * last))
        )
    return ready[-1]


def solution(mesh):
    placed = (
        P("row", "col"),
        P("row", None, None, None),
        P(),
        P("row", "col"),
        P("row", "col"),
        P("row"),
    )
    return jax.shard_map(
        forecast, mesh=mesh, in_specs=placed, out_specs=P("row", "col"), check_vma=False
    )
```

profile of v0, /device:TPU:0, one launch (start us, length us, event | category | flops | bytes accessed | tf_op | source)
XLA Modules:
  0.0 77.4 jit_solution(9244108045760584294)
XLA Ops:
  0.0 5.0 %collective-permute-start = (bf16[4,7,128,128]{3,2,1,0:T(8,128)(2,1)}, bf16[4,7,128,128]{3,2,1,0:T(8,128)(2,1)S(1)}, u32[]{:S(2)}, u32[]{:S(2)}) collective-permute-start(bf16[4,7,128,128]{3,2,1,0:T(8,128)(2,1)} %refs_0_.1), channel_id=1, source_target_pairs={{0,8},{4,20},{13,5},{9,25},{22,30},{18,2},{27,19},{31,15}} | collective-permute-start | bytes 2752520 | tf_op jit(solution)/shard_map/ppermute | solution.py:262
  5.1 1.3 %collective-permute-start.2 = (bf16[4,7,128,128]{3,2,1,0:T(8,128)(2,1)}, bf16[4,7,128,128]{3,2,1,0:T(8,128)(2,1)S(1)}, u32[]{:S(2)}, u32[]{:S(2)}) collective-permute-start(bf16[4,7,128,128]{3,2,1,0:T(8,128)(2,1)} %refs_0_.1), channel_id=1, source_target_pairs={{0,16},{4,12},{13,29},{9,1},{22,6},{18,26},{27,11},{31,23}} | collective-permute-start | bytes 2752520 | tf_op jit(solution)/shard_map/ppermute | solution.py:262
  6.4 19.4 %collective-permute-done.refs_1_ = bf16[4,7,128,128]{3,2,1,0:T(8,128)(2,1)S(1)} collective-permute-done((bf16[4,7,128,128]{3,2,1,0:T(8,128)(2,1)}, bf16[4,7,128,128]{3,2,1,0:T(8,128)(2,1)S(1)}, u32[]{:S(2)}, u32[]{:S(2)}) %collective-permute-start) | collective-permute-done | bytes 917536 | tf_op jit(solution)/shard_map/ppermute | solution.py:262
  25.8 0.7 collective-permute-start.1
  26.5 1.3 %fusion = (bf16[256,1024]{1,0:T(8,128)(2,1)S(1)}, bf16[256,1024]{1,0:T(8,128)(2,1)S(1)}) fusion(bf16[512,1024]{1,0:T(8,128)(2,1)} %param.6), kind=kLoop, calls=%fused_computation | loop fusion | bytes 2097152 | tf_op jit(solution)/shard_map/slice | solution.py:237
  27.8 1.3 %collective-permute-start.7 = (bf16[256,1024]{1,0:T(8,128)(2,1)S(1)}, bf16[256,1024]{1,0:T(8,128)(2,1)S(1)}, u32[]{:S(2)}, u32[]{:S(2)}) collective-permute-start(bf16[256,1024]{1,0:T(8,128)(2,1)S(1)} %get-tuple-element.17.bottom_hbm), channel_id=1, source_target_pairs={{12,28},{16,0},{13,29},{17,1},{14,30},{18,2},{15,31},{19,3}} | collective-permute-start | bytes 1572872 | tf_op jit(solution)/shard_map/ppermute | solution.py:255
  29.1 0.1 collective-permute-start.4
  29.2 0.7 collective-permute-start.5
  29.9 8.9 %collective-permute-done.7 = bf16[256,1024]{1,0:T(8,128)(2,1)S(1)} collective-permute-done((bf16[256,1024]{1,0:T(8,128)(2,1)S(1)}, bf16[256,1024]{1,0:T(8,128)(2,1)S(1)}, u32[]{:S(2)}, u32[]{:S(2)}) %collective-permute-start.7) | collective-permute-done | bytes 524320 | tf_op jit(solution)/shard_map/ppermute | solution.py:255
  38.9 0.8 %collective-permute-start.6 = (bf16[256,1024]{1,0:T(8,128)(2,1)S(1)}, bf16[256,1024]{1,0:T(8,128)(2,1)S(1)}, u32[]{:S(2)}, u32[]{:S(2)}) collective-permute-start(bf16[256,1024]{1,0:T(8,128)(2,1)S(1)} %get-tuple-element.18.top_hbm), channel_id=1, source_target_pairs={{12,16},{16,12},{13,17},{17,13},{14,18},{18,14},{15,19},{19,15}} | collective-permute-start | bytes 1572872 | tf_op jit(solution)/shard_map/ppermute | solution.py:254
  39.7 0.0 collective-permute-done.2.refs_3_
  39.7 3.9 %collective-permute-start.8 = (bf16[256,1024]{1,0:T(8,128)(2,1)S(1)}, bf16[256,1024]{1,0:T(8,128)(2,1)S(1)}, u32[]{:S(2)}, u32[]{:S(2)}) collective-permute-start(bf16[256,1024]{1,0:T(8,128)(2,1)S(1)} %collective-permute-done.7), channel_id=1, source_target_pairs={{28,16},{0,12},{29,17},{1,13},{30,18},{2,14},{31,19},{3,15}} | collective-permute-start | bytes 1572872 | tf_op jit(solution)/shard_map/ppermute | solution.py:256
  43.6 0.0 collective-permute-done.1.refs_2_
  43.6 1.3 %pick.1.f_ref = bf16[4,7,128,128]{3,2,1,0:T(8,128)(2,1)S(1)} custom-call(bf16[4,7,128,128]{3,2,1,0:T(8,128)(2,1)S(1)} %copy-done.1, bf16[4,7,128,128]{3,2,1,0:T(8,128)(2,1)S(1)} %collective-permute-done.refs_1_, bf16[4,7,128,128]{3,2,1,0:T(8,128)(2,1)S(1)} %collective-permute-done.1.refs_2_, bf16[4,7,128,128]{3,2,1,0:T(8,128)(2,1)S(1)} %collective-permute-done.2.refs_3_), custom_call_target="tpu_custom_call" | custom-call | tf_op jit(solution)/shard_map/pick/pallas_call | solution.py:284
  44.9 0.1 collective-permute-start.3
  45.0 0.2 fetch.1
  45.2 5.6 %collective-permute-done.8.refs_1_ = bf16[256,1024]{1,0:T(8,128)(2,1)S(1)} collective-permute-done((bf16[256,1024]{1,0:T(8,128)(2,1)S(1)}, bf16[256,1024]{1,0:T(8,128)(2,1)S(1)}, u32[]{:S(2)}, u32[]{:S(2)}) %collective-permute-start.8) | collective-permute-done | bytes 524320 | tf_op jit(solution)/shard_map/ppermute | solution.py:256
  50.8 0.0 copy-start.3
  50.9 2.2 %stage1.1 = (bf16[512,512]{1,0:T(8,128)(2,1)S(1)}, bf16[512,512]{1,0:T(8,128)(2,1)S(1)}) custom-call(s32[7,32]{1,0:T(8,128)S(1)} %get-tuple-element.11.cols_ref, bf16[4,7,128,128]{3,2,1,0:T(8,128)(2,1)S(1)} %get-tuple-element.12.f_ref, bf16[256,1024]{1,0:T(8,128)(2,1)S(1)} %get-tuple-element.18.top_hbm, bf16[256,1024]{1,0:T(8,128)(2,1)S(1)} %get-tuple-element.17.bottom_hbm, ...), custom_call_target="tpu_custom_call" | custom-call | tf_op jit(solution)/shard_map/stage1/pallas_call | solution.py:265
  53.1 0.7 collective-permute-start.10
  53.8 8.4 %collective-permute-start.9 = (bf16[512,512]{1,0:T(8,128)(2,1)S(1)}, bf16[512,512]{1,0:T(8,128)(2,1)S(1)}, u32[]{:S(2)}, u32[]{:S(2)}) collective-permute-start(bf16[512,512]{1,0:T(8,128)(2,1)S(1)} %get-tuple-element.13.refs_1_), channel_id=1, source_target_pairs={{0,1},{2,3},{1,0},{3,2},{4,5},{6,7},{5,4},{7,6},{8,9},{10,11},{9,8... | collective-permute-start | bytes 1572872 | tf_op jit(solution)/shard_map/ppermute | solution.py:281
  62.1 10.3 %collective-permute-done.9.refs_0_ = bf16[512,512]{1,0:T(8,128)(2,1)S(1)} collective-permute-done((bf16[512,512]{1,0:T(8,128)(2,1)S(1)}, bf16[512,512]{1,0:T(8,128)(2,1)S(1)}, u32[]{:S(2)}, u32[]{:S(2)}) %collective-permute-start.9) | collective-permute-done | bytes 524320 | tf_op jit(solution)/shard_map/ppermute | solution.py:281
  72.4 2.3 %stage2.1 = (f32[4,512,128]{2,1,0:T(8,128)S(1)}, bf16[512,2048]{1,0:T(8,128)(2,1)S(1)}) custom-call(s32[7,32]{1,0:T(8,128)S(1)} %get-tuple-element.11.cols_ref, s32[4,8]{1,0:T(4,128)S(1)} %copy-done.2, f32[4,128]{1,0:T(4,128)S(1)} %bitcast.2, bf16[512,1024]{1,0:T(8,128)(2,1)S(1)} %copy-done, bf16[4,7,128,128]{3,2,1,0:T(8,128)(2,1)S(1)} %pick.1.f_ref, ...), custom_call_target="tpu_custom_call" | custom-call | tf_op jit(solution)/shard_map/stage2/pallas_call | solution.py:303
  74.7 2.7 %stage3.1 = f32[512,1024]{1,0:T(8,128)} custom-call(s32[7,32]{1,0:T(8,128)S(1)} %get-tuple-element.11.cols_ref, s32[4,8]{1,0:T(4,128)S(1)} %copy-done.2, f32[4,128]{1,0:T(4,128)S(1)} %bitcast.3, bf16[512,1024]{1,0:T(8,128)(2,1)S(1)} %copy-done, bf16[4,7,128,128]{3,2,1,0:T(8,128)(2,1)S(1)} %collective-permute-done.3.f_ref, ...), custom_call_target="tpu_custom_call" | custom-call | tf_op jit(solution)/shard_map/stage3/pallas_call | solution.py:318
  (16 shorter events, 0.0 us)
Async XLA Ops:
  0.0 43.6 %copy-start.1 = (bf16[4,7,128,128]{3,2,1,0:T(8,128)(2,1)S(1)}, bf16[4,7,128,128]{3,2,1,0:T(8,128)(2,1)}, u32[]{:S(2)}) copy-start(bf16[4,7,128,128]{3,2,1,0:T(8,128)(2,1)} %refs_0_.1) | copy-start | bytes 2752516
  0.0 29.1 %copy-start.5 = (bf16[512,1024]{1,0:T(8,128)(2,1)S(1)}, bf16[512,1024]{1,0:T(8,128)(2,1)}, u32[]{:S(2)}) copy-start(bf16[512,1024]{1,0:T(8,128)(2,1)} %param.6) | copy-start | bytes 3145732
  0.0 25.8 %collective-permute-start = (bf16[4,7,128,128]{3,2,1,0:T(8,128)(2,1)}, bf16[4,7,128,128]{3,2,1,0:T(8,128)(2,1)S(1)}, u32[]{:S(2)}, u32[]{:S(2)}) collective-permute-start(bf16[4,7,128,128]{3,2,1,0:T(8,128)(2,1)} %refs_0_.1), channel_id=1, source_target_pairs={{0,8},{4,20},{13,5},{9,25},{22,30},{18,2},{27,19},{31,15}} | collective-permute-start | bytes 2752520 | tf_op jit(solution)/shard_map/ppermute | solution.py:262
  5.1 34.6 %collective-permute-start.2 = (bf16[4,7,128,128]{3,2,1,0:T(8,128)(2,1)}, bf16[4,7,128,128]{3,2,1,0:T(8,128)(2,1)S(1)}, u32[]{:S(2)}, u32[]{:S(2)}) collective-permute-start(bf16[4,7,128,128]{3,2,1,0:T(8,128)(2,1)} %refs_0_.1), channel_id=1, source_target_pairs={{0,16},{4,12},{13,29},{9,1},{22,6},{18,26},{27,11},{31,23}} | collective-permute-start | bytes 2752520 | tf_op jit(solution)/shard_map/ppermute | solution.py:262
  25.8 17.8 %collective-permute-start.1 = (bf16[4,7,128,128]{3,2,1,0:T(8,128)(2,1)S(1)}, bf16[4,7,128,128]{3,2,1,0:T(8,128)(2,1)S(1)}, u32[]{:S(2)}, u32[]{:S(2)}) collective-permute-start(bf16[4,7,128,128]{3,2,1,0:T(8,128)(2,1)S(1)} %collective-permute-done.refs_1_), channel_id=1, source_target_pairs={{8,24},{20,28},{5,21},{25,17},{30,14},{2,10},{19,3},{15,7}} | collective-permute-start | bytes 2752520 | tf_op jit(solution)/shard_map/ppermute | solution.py:262
  27.8 11.1 %collective-permute-start.7 = (bf16[256,1024]{1,0:T(8,128)(2,1)S(1)}, bf16[256,1024]{1,0:T(8,128)(2,1)S(1)}, u32[]{:S(2)}, u32[]{:S(2)}) collective-permute-start(bf16[256,1024]{1,0:T(8,128)(2,1)S(1)} %get-tuple-element.17.bottom_hbm), channel_id=1, source_target_pairs={{12,28},{16,0},{13,29},{17,1},{14,30},{18,2},{15,31},{19,3}} | collective-permute-start | bytes 1572872 | tf_op jit(solution)/shard_map/ppermute | solution.py:255
  29.1 21.7 %collective-permute-start.4 = (bf16[512,1024]{1,0:T(8,128)(2,1)S(1)}, bf16[512,1024]{1,0:T(8,128)(2,1)S(1)}, u32[]{:S(2)}, u32[]{:S(2)}) collective-permute-start(bf16[512,1024]{1,0:T(8,128)(2,1)S(1)} %copy-done.5), channel_id=1, source_target_pairs={{0,4},{8,12},{16,20},{24,28},{4,0},{12,8},{20,16},{28,24},{1,5},{9... | collective-permute-start | bytes 3145736 | tf_op jit(solution)/shard_map/ppermute | solution.py:258
  29.2 21.7 %collective-permute-start.5 = (bf16[512,1024]{1,0:T(8,128)(2,1)S(1)}, bf16[512,1024]{1,0:T(8,128)(2,1)S(1)}, u32[]{:S(2)}, u32[]{:S(2)}) collective-permute-start(bf16[512,1024]{1,0:T(8,128)(2,1)S(1)} %copy-done.5), channel_id=1, source_target_pairs={{4,8},{20,24},{8,4},{24,20},{5,9},{21,25},{9,5},{25,21},{6,10},{22... | collective-permute-start | bytes 3145736 | tf_op jit(solution)/shard_map/ppermute | solution.py:259
  38.9 6.1 %copy-start.4 = (s32[32,7]{0,1:T(8,128)S(1)}, s32[32,7]{0,1:T(8,128)}, u32[]{:S(2)}) copy-start(s32[32,7]{0,1:T(8,128)} %param.8) | copy-start | bytes 2692
  38.9 6.4 %collective-permute-start.6 = (bf16[256,1024]{1,0:T(8,128)(2,1)S(1)}, bf16[256,1024]{1,0:T(8,128)(2,1)S(1)}, u32[]{:S(2)}, u32[]{:S(2)}) collective-permute-start(bf16[256,1024]{1,0:T(8,128)(2,1)S(1)} %get-tuple-element.18.top_hbm), channel_id=1, source_target_pairs={{12,16},{16,12},{13,17},{17,13},{14,18},{18,14},{15,19},{19,15}} | collective-permute-start | bytes 1572872 | tf_op jit(solution)/shard_map/ppermute | solution.py:254
  39.7 11.1 %collective-permute-start.8 = (bf16[256,1024]{1,0:T(8,128)(2,1)S(1)}, bf16[256,1024]{1,0:T(8,128)(2,1)S(1)}, u32[]{:S(2)}, u32[]{:S(2)}) collective-permute-start(bf16[256,1024]{1,0:T(8,128)(2,1)S(1)} %collective-permute-done.7), channel_id=1, source_target_pairs={{28,16},{0,12},{29,17},{1,13},{30,18},{2,14},{31,19},{3,15}} | collective-permute-start | bytes 1572872 | tf_op jit(solution)/shard_map/ppermute | solution.py:256
  44.9 29.8 %collective-permute-start.3 = (bf16[4,7,128,128]{3,2,1,0:T(8,128)(2,1)S(1)}, bf16[4,7,128,128]{3,2,1,0:T(8,128)(2,1)S(1)}, u32[]{:S(2)}, u32[]{:S(2)}) collective-permute-start(bf16[4,7,128,128]{3,2,1,0:T(8,128)(2,1)S(1)} %pick.1.f_ref), channel_id=1, source_target_pairs={{4,0},{0,4},{12,8},{8,12},{20,16},{16,20},{28,24},{24,28},{5,1},{1... | collective-permute-start | bytes 2752520 | tf_op jit(solution)/shard_map/ppermute | solution.py:316
  50.8 21.5 %copy-start = (bf16[512,1024]{1,0:T(8,128)(2,1)S(1)}, bf16[512,1024]{1,0:T(8,128)(2,1)}, u32[]{:S(2)}) copy-start(bf16[512,1024]{1,0:T(8,128)(2,1)} %w_ref.3) | copy-start | bytes 3145732
  50.8 21.5 %copy-start.2 = (s32[4,8]{1,0:T(4,128)S(1)}, s32[4,8]{1,0:T(4,128)}, u32[]{:S(2)}) copy-start(s32[4,8]{1,0:T(4,128)} %mask_ref.3) | copy-start | bytes 388
  50.8 21.5 %copy-start.3 = (f32[512]{0:T(512)S(1)}, f32[512]{0:T(512)}, u32[]{:S(2)}) copy-start(f32[512]{0:T(512)} %param.11) | copy-start | bytes 6148
  53.1 9.1 %collective-permute-start.10 = (bf16[512,512]{1,0:T(8,128)(2,1)S(1)}, bf16[512,512]{1,0:T(8,128)(2,1)S(1)}, u32[]{:S(2)}, u32[]{:S(2)}) collective-permute-start(bf16[512,512]{1,0:T(8,128)(2,1)S(1)} %get-tuple-element.14.refs_2_), channel_id=1, source_target_pairs={{1,2},{2,1},{0,0},{3,3},{5,6},{6,5},{4,4},{7,7},{9,10},{10,9},{8,8... | collective-permute-start | bytes 1572872 | tf_op jit(solution)/shard_map/ppermute | solution.py:282
  53.8 18.6 %collective-permute-start.9 = (bf16[512,512]{1,0:T(8,128)(2,1)S(1)}, bf16[512,512]{1,0:T(8,128)(2,1)S(1)}, u32[]{:S(2)}, u32[]{:S(2)}) collective-permute-start(bf16[512,512]{1,0:T(8,128)(2,1)S(1)} %get-tuple-element.13.refs_1_), channel_id=1, source_target_pairs={{0,1},{2,3},{1,0},{3,2},{4,5},{6,7},{5,4},{7,6},{8,9},{10,11},{9,8... | collective-permute-start | bytes 1572872 | tf_op jit(solution)/shard_map/ppermute | solution.py:281
where the time goes:
time: 78.5 us; the launch traced here: 77.4 us
  waiting for transfers between devices  44.2 us (56%)
  starting transfers between devices  23 us (29%)
  Pallas kernels  8.65 us (11%)
  local copies, waits for them, and re-layouts  1.29 us (2%)
    ppermute x3, waiting for transfers between devices, forecast(): held.append(lax.ppermute(held[source], ('row', 'col'), pairs))  19.4 us
    ppermute x1, waiting for transfers between devices, forecast(): nearer = lax.ppermute(first, 'col', inner_pairs)  10.3 us
    ppermute x1, waiting for transfers between devices, forecast(): turn = lax.ppermute(bottom, 'row', [(upper, rows - 1), (lower, 0)])  8.95 us
    ppermute x1, starting transfers between devices, forecast(): nearer = lax.ppermute(first, 'col', inner_pairs)  8.36 us
    ppermute x3, starting transfers between devices, forecast(): held.append(lax.ppermute(held[source], ('row', 'col'), pairs))  7.1 us
    ppermute x1, waiting for transfers between devices, forecast(): turned = lax.ppermute(turn, 'row', [(rows - 1, lower), (0, upper)])  5.61 us
    ppermute x1, starting transfers between devices, forecast(): turned = lax.ppermute(turn, 'row', [(rows - 1, lower), (0, upper)])  3.88 us
    pallas_call x1, Pallas kernels, forecast(): pl.pallas_call(functools.partial(stage2_kernel, fan, turn), out_shape=jax...  2.67 us
  transfers between devices with their start and end apart: 11, of which 4 were waited for; matrix products, arithmetic and copies ran while one was open for 2% of the time, Pallas kernels for 8%

commit v1 on v0

--- a/solution.py
+++ b/solution.py
@@ -44,10 +44,9 @@
     first, relayed, second = [], [], []
     for c in range(cols):
         near, side, far = c ^ 1, c ^ 2, c ^ 3
-        i, j = (1, 0) if c in (1, 2) else (0, 1)
-        first += [(at(c, i, c), at(near, i, c)), (at(c, j, c), at(side, j, c))]
-        relayed += [(at(near, i, c), at(far, i, c)), (at(side, j, c), at(far, j, c))]
-        second += [(at(c, i, c), at(side, i, c)), (at(c, j, c), at(near, j, c))]
+        first += [(at(c, 0, c), at(near, 0, c)), (at(c, 1, c), at(side, 1, c))]
+        relayed += [(at(near, 0, c), at(far, 0, c)), (at(side, 1, c), at(far, 1, c))]
+        second += [(at(c, 0, c), at(side, 0, c)), (at(c, 1, c), at(near, 1, c))]
     return [(0, first), (1, relayed), (0, second)]
 
 
@@ -259,7 +258,9 @@
     outer = lax.ppermute(p_cov, "row", outer_pairs)
     held = [f_blocks]
     for source, pairs in group_plan(rows, cols):
-        held.append(lax.ppermute(held[source], ("row", "col"), pairs))
+        busy = {i for pair in pairs for i in pair}
+        idle = [(i, i) for i in range(rows * cols) if i not in busy]
+        held.append(lax.ppermute(held[source], ("row", "col"), pairs + idle))
 
     half = jax.ShapeDtypeStruct((tall, halo), jnp.bfloat16)
     first, second = pl.pallas_call(
@@ -284,7 +285,7 @@
     mine = pl.pallas_call(
         functools.partial(pick_kernel, holder_table(rows, cols)),
         out_shape=jax.ShapeDtypeStruct(f_blocks.shape, f_blocks.dtype),
-        in_specs=[vmem] * len(held),
+        in_specs=[hbm] * len(held),
         out_specs=vmem,
         scratch_shapes=[pltpu.SemaphoreType.DMA((block_rows,))],
         compiler_params=pltpu.CompilerParams(vmem_limit_bytes=4 * 2**20),

time: 78.5 us -> 74.2 us (0.945)
  the two profiles are of different devices: /device:TPU:0 before, /device:TPU:23 now
where the time goes in v1:
time: 74.2 us; the launch traced here: 73.9 us
  starting transfers between devices  44.6 us (60%)
  waiting for transfers between devices  19.1 us (26%)
  Pallas kernels  8.67 us (12%)
  local copies, waits for them, and re-layouts  1.3 us (2%)
    ppermute x1, starting transfers between devices, forecast(): inner = lax.ppermute(p_cov, 'row', inner_pairs)  22.3 us
    ppermute x1, starting transfers between devices, forecast(): turned = lax.ppermute(turn, 'row', [(rows - 1, lower), (0, upper)])  8.37 us
    ppermute x1, waiting for transfers between devices, forecast(): further = lax.ppermute(second, 'col', outer_pairs)  7.98 us
    ppermute x1, waiting for transfers between devices, forecast(): turned = lax.ppermute(turn, 'row', [(rows - 1, lower), (0, upper)])  7.98 us
    ppermute x3, starting transfers between devices, forecast(): held.append(lax.ppermute(held[source], ('row', 'col'), pairs + idle))  3.96 us
    ppermute x1, starting transfers between devices, forecast(): further = lax.ppermute(second, 'col', outer_pairs)  3.92 us
    ppermute x1, starting transfers between devices, forecast(): nearer = lax.ppermute(first, 'col', inner_pairs)  3.3 us
    ppermute x1, waiting for transfers between devices, forecast(): nearer = lax.ppermute(first, 'col', inner_pairs)  3.15 us
  transfers between devices with their start and end apart: 11, of which 3 were waited for; matrix products, arithmetic and copies ran while one was open for 2% of the time, Pallas kernels for 8%

profile of v1, /device:TPU:23, one launch (start us, length us, event | category | flops | bytes accessed | tf_op | source)
XLA Modules:
  0.0 73.9 jit_solution(3739344248900091617)
XLA Ops:
  0.0 2.0 %collective-permute-start = (bf16[4,7,128,128]{3,2,1,0:T(8,128)(2,1)}, bf16[4,7,128,128]{3,2,1,0:T(8,128)(2,1)S(1)}, u32[]{:S(2)}, u32[]{:S(2)}) collective-permute-start(bf16[4,7,128,128]{3,2,1,0:T(8,128)(2,1)} %refs_0_.1), channel_id=1, source_target_pairs={{0,8},{4,20},{9,1},{13,29},{18,26},{22,6},{27,19},{31,15},{2,2},{3... | collective-permute-start | bytes 2752520 | tf_op jit(solution)/shard_map/ppermute | solution.py:263
  2.0 1.3 %collective-permute-start.2 = (bf16[4,7,128,128]{3,2,1,0:T(8,128)(2,1)}, bf16[4,7,128,128]{3,2,1,0:T(8,128)(2,1)S(1)}, u32[]{:S(2)}, u32[]{:S(2)}) collective-permute-start(bf16[4,7,128,128]{3,2,1,0:T(8,128)(2,1)} %refs_0_.1), channel_id=1, source_target_pairs={{0,16},{4,12},{9,25},{13,5},{18,2},{22,30},{27,11},{31,23},{1,1},{... | collective-permute-start | bytes 2752520 | tf_op jit(solution)/shard_map/ppermute | solution.py:263
  3.2 0.0 collective-permute-done.refs_1_
  3.3 0.7 collective-permute-start.1
  4.0 1.3 %fusion = (bf16[256,1024]{1,0:T(8,128)(2,1)S(1)}, bf16[256,1024]{1,0:T(8,128)(2,1)S(1)}) fusion(bf16[512,1024]{1,0:T(8,128)(2,1)} %param.6), kind=kLoop, calls=%fused_computation | loop fusion | bytes 2097152 | tf_op jit(solution)/shard_map/slice | solution.py:236
  5.3 1.3 %collective-permute-start.7 = (bf16[256,1024]{1,0:T(8,128)(2,1)S(1)}, bf16[256,1024]{1,0:T(8,128)(2,1)S(1)}, u32[]{:S(2)}, u32[]{:S(2)}) collective-permute-start(bf16[256,1024]{1,0:T(8,128)(2,1)S(1)} %get-tuple-element.17.bottom_hbm), channel_id=1, source_target_pairs={{12,28},{16,0},{13,29},{17,1},{14,30},{18,2},{15,31},{19,3}} | collective-permute-start | bytes 1572872 | tf_op jit(solution)/shard_map/ppermute | solution.py:254
  6.6 22.3 %collective-permute-start.4 = (bf16[512,1024]{1,0:T(8,128)(2,1)S(1)}, bf16[512,1024]{1,0:T(8,128)(2,1)S(1)}, u32[]{:S(2)}, u32[]{:S(2)}) collective-permute-start(bf16[512,1024]{1,0:T(8,128)(2,1)S(1)} %copy-done.5), channel_id=1, source_target_pairs={{0,4},{8,12},{16,20},{24,28},{4,0},{12,8},{20,16},{28,24},{1,5},{9... | collective-permute-start | bytes 3145736 | tf_op jit(solution)/shard_map/ppermute | solution.py:257
  28.8 0.7 collective-permute-start.5
  29.6 0.0 copy-start.4
  29.6 0.7 collective-permute-start.6
  30.3 8.4 %collective-permute-start.8 = (bf16[256,1024]{1,0:T(8,128)(2,1)S(1)}, bf16[256,1024]{1,0:T(8,128)(2,1)S(1)}, u32[]{:S(2)}, u32[]{:S(2)}) collective-permute-start(bf16[256,1024]{1,0:T(8,128)(2,1)S(1)} %collective-permute-done.7), channel_id=1, source_target_pairs={{28,16},{0,12},{29,17},{1,13},{30,18},{2,14},{31,19},{3,15}} | collective-permute-start | bytes 1572872 | tf_op jit(solution)/shard_map/ppermute | solution.py:255
  38.7 1.3 %pick.1.f_ref = bf16[4,7,128,128]{3,2,1,0:T(8,128)(2,1)S(1)} custom-call(bf16[4,7,128,128]{3,2,1,0:T(8,128)(2,1)S(1)} %copy-done.1, bf16[4,7,128,128]{3,2,1,0:T(8,128)(2,1)S(1)} %collective-permute-done.refs_1_, bf16[4,7,128,128]{3,2,1,0:T(8,128)(2,1)S(1)} %collective-permute-done.1.refs_2_, bf16[4,7,128,128]{3,2,1,0:T(8,128)(2,1)S(1)} %collective-permute-done.2.refs_3_), custom_call_target="tpu_custom_call" | custom-call | tf_op jit(solution)/shard_map/pick/pallas_call | solution.py:285
  40.0 0.1 collective-permute-start.3
  40.1 0.2 fetch.1
  40.3 0.0 collective-permute-done.6.refs_0_
  40.3 8.0 %collective-permute-done.8.refs_1_ = bf16[256,1024]{1,0:T(8,128)(2,1)S(1)} collective-permute-done((bf16[256,1024]{1,0:T(8,128)(2,1)S(1)}, bf16[256,1024]{1,0:T(8,128)(2,1)S(1)}, u32[]{:S(2)}, u32[]{:S(2)}) %collective-permute-start.8) | collective-permute-done | bytes 524320 | tf_op jit(solution)/shard_map/ppermute | solution.py:255
  48.3 0.0 copy-start.3
  48.3 2.2 %stage1.1 = (bf16[512,512]{1,0:T(8,128)(2,1)S(1)}, bf16[512,512]{1,0:T(8,128)(2,1)S(1)}) custom-call(s32[7,32]{1,0:T(8,128)S(1)} %get-tuple-element.11.cols_ref, bf16[4,7,128,128]{3,2,1,0:T(8,128)(2,1)S(1)} %get-tuple-element.12.f_ref, bf16[256,1024]{1,0:T(8,128)(2,1)S(1)} %get-tuple-element.18.top_hbm, bf16[256,1024]{1,0:T(8,128)(2,1)S(1)} %get-tuple-element.17.bottom_hbm, ...), custom_call_target="tpu_custom_call" | custom-call | tf_op jit(solution)/shard_map/stage1/pallas_call | solution.py:266
  50.5 3.9 %collective-permute-start.10 = (bf16[512,512]{1,0:T(8,128)(2,1)S(1)}, bf16[512,512]{1,0:T(8,128)(2,1)S(1)}, u32[]{:S(2)}, u32[]{:S(2)}) collective-permute-start(bf16[512,512]{1,0:T(8,128)(2,1)S(1)} %get-tuple-element.14.refs_2_), channel_id=1, source_target_pairs={{1,2},{2,1},{0,0},{3,3},{5,6},{6,5},{4,4},{7,7},{9,10},{10,9},{8,8... | collective-permute-start | bytes 1572872 | tf_op jit(solution)/shard_map/ppermute | solution.py:283
  54.5 3.3 %collective-permute-start.9 = (bf16[512,512]{1,0:T(8,128)(2,1)S(1)}, bf16[512,512]{1,0:T(8,128)(2,1)S(1)}, u32[]{:S(2)}, u32[]{:S(2)}) collective-permute-start(bf16[512,512]{1,0:T(8,128)(2,1)S(1)} %get-tuple-element.13.refs_1_), channel_id=1, source_target_pairs={{0,1},{2,3},{1,0},{3,2},{4,5},{6,7},{5,4},{7,6},{8,9},{10,11},{9,8... | collective-permute-start | bytes 1572872 | tf_op jit(solution)/shard_map/ppermute | solution.py:282
  57.8 8.0 %collective-permute-done.10.refs_3_ = bf16[512,512]{1,0:T(8,128)(2,1)S(1)} collective-permute-done((bf16[512,512]{1,0:T(8,128)(2,1)S(1)}, bf16[512,512]{1,0:T(8,128)(2,1)S(1)}, u32[]{:S(2)}, u32[]{:S(2)}) %collective-permute-start.10) | collective-permute-done | bytes 524320 | tf_op jit(solution)/shard_map/ppermute | solution.py:283
  65.7 3.1 %collective-permute-done.9.refs_0_ = bf16[512,512]{1,0:T(8,128)(2,1)S(1)} collective-permute-done((bf16[512,512]{1,0:T(8,128)(2,1)S(1)}, bf16[512,512]{1,0:T(8,128)(2,1)S(1)}, u32[]{:S(2)}, u32[]{:S(2)}) %collective-permute-start.9) | collective-permute-done | bytes 524320 | tf_op jit(solution)/shard_map/ppermute | solution.py:282
  68.9 2.3 %stage2.1 = (f32[4,512,128]{2,1,0:T(8,128)S(1)}, bf16[512,2048]{1,0:T(8,128)(2,1)S(1)}) custom-call(s32[7,32]{1,0:T(8,128)S(1)} %get-tuple-element.11.cols_ref, s32[4,8]{1,0:T(4,128)S(1)} %copy-done.2, f32[4,128]{1,0:T(4,128)S(1)} %bitcast.2, bf16[512,1024]{1,0:T(8,128)(2,1)S(1)} %copy-done, bf16[4,7,128,128]{3,2,1,0:T(8,128)(2,1)S(1)} %pick.1.f_ref, ...), custom_call_target="tpu_custom_call" | custom-call | tf_op jit(solution)/shard_map/stage2/pallas_call | solution.py:304
  71.2 2.7 %stage3.1 = f32[512,1024]{1,0:T(8,128)} custom-call(s32[7,32]{1,0:T(8,128)S(1)} %get-tuple-element.11.cols_ref, s32[4,8]{1,0:T(4,128)S(1)} %copy-done.2, f32[4,128]{1,0:T(4,128)S(1)} %bitcast.3, bf16[512,1024]{1,0:T(8,128)(2,1)S(1)} %copy-done, bf16[4,7,128,128]{3,2,1,0:T(8,128)(2,1)S(1)} %collective-permute-done.3.f_ref, ...), custom_call_target="tpu_custom_call" | custom-call | tf_op jit(solution)/shard_map/stage3/pallas_call | solution.py:319
  (16 shorter events, 0.0 us)
Async XLA Ops:
  0.0 38.7 %copy-start.1 = (bf16[4,7,128,128]{3,2,1,0:T(8,128)(2,1)S(1)}, bf16[4,7,128,128]{3,2,1,0:T(8,128)(2,1)}, u32[]{:S(2)}) copy-start(bf16[4,7,128,128]{3,2,1,0:T(8,128)(2,1)} %refs_0_.1) | copy-start | bytes 2752516
  0.0 6.6 %copy-start.5 = (bf16[512,1024]{1,0:T(8,128)(2,1)S(1)}, bf16[512,1024]{1,0:T(8,128)(2,1)}, u32[]{:S(2)}) copy-start(bf16[512,1024]{1,0:T(8,128)(2,1)} %param.6) | copy-start | bytes 3145732
  0.0 3.2 %collective-permute-start = (bf16[4,7,128,128]{3,2,1,0:T(8,128)(2,1)}, bf16[4,7,128,128]{3,2,1,0:T(8,128)(2,1)S(1)}, u32[]{:S(2)}, u32[]{:S(2)}) collective-permute-start(bf16[4,7,128,128]{3,2,1,0:T(8,128)(2,1)} %refs_0_.1), channel_id=1, source_target_pairs={{0,8},{4,20},{9,1},{13,29},{18,26},{22,6},{27,19},{31,15},{2,2},{3... | collective-permute-start | bytes 2752520 | tf_op jit(solution)/shard_map/ppermute | solution.py:263
  2.0 28.3 %collective-permute-start.2 = (bf16[4,7,128,128]{3,2,1,0:T(8,128)(2,1)}, bf16[4,7,128,128]{3,2,1,0:T(8,128)(2,1)S(1)}, u32[]{:S(2)}, u32[]{:S(2)}) collective-permute-start(bf16[4,7,128,128]{3,2,1,0:T(8,128)(2,1)} %refs_0_.1), channel_id=1, source_target_pairs={{0,16},{4,12},{9,25},{13,5},{18,2},{22,30},{27,11},{31,23},{1,1},{... | collective-permute-start | bytes 2752520 | tf_op jit(solution)/shard_map/ppermute | solution.py:263
  3.3 35.4 %collective-permute-start.1 = (bf16[4,7,128,128]{3,2,1,0:T(8,128)(2,1)S(1)}, bf16[4,7,128,128]{3,2,1,0:T(8,128)(2,1)S(1)}, u32[]{:S(2)}, u32[]{:S(2)}) collective-permute-start(bf16[4,7,128,128]{3,2,1,0:T(8,128)(2,1)S(1)} %collective-permute-done.refs_1_), channel_id=1, source_target_pairs={{8,24},{20,28},{1,17},{29,21},{26,10},{6,14},{19,3},{15,7},{0,0},{... | collective-permute-start | bytes 2752520 | tf_op jit(solution)/shard_map/ppermute | solution.py:263
  5.3 24.3 %collective-permute-start.7 = (bf16[256,1024]{1,0:T(8,128)(2,1)S(1)}, bf16[256,1024]{1,0:T(8,128)(2,1)S(1)}, u32[]{:S(2)}, u32[]{:S(2)}) collective-permute-start(bf16[256,1024]{1,0:T(8,128)(2,1)S(1)} %get-tuple-element.17.bottom_hbm), channel_id=1, source_target_pairs={{12,28},{16,0},{13,29},{17,1},{14,30},{18,2},{15,31},{19,3}} | collective-permute-start | bytes 1572872 | tf_op jit(solution)/shard_map/ppermute | solution.py:254
  6.6 41.7 %collective-permute-start.4 = (bf16[512,1024]{1,0:T(8,128)(2,1)S(1)}, bf16[512,1024]{1,0:T(8,128)(2,1)S(1)}, u32[]{:S(2)}, u32[]{:S(2)}) collective-permute-start(bf16[512,1024]{1,0:T(8,128)(2,1)S(1)} %copy-done.5), channel_id=1, source_target_pairs={{0,4},{8,12},{16,20},{24,28},{4,0},{12,8},{20,16},{28,24},{1,5},{9... | collective-permute-start | bytes 3145736 | tf_op jit(solution)/shard_map/ppermute | solution.py:257
  28.8 19.5 %collective-permute-start.5 = (bf16[512,1024]{1,0:T(8,128)(2,1)S(1)}, bf16[512,1024]{1,0:T(8,128)(2,1)S(1)}, u32[]{:S(2)}, u32[]{:S(2)}) collective-permute-start(bf16[512,1024]{1,0:T(8,128)(2,1)S(1)} %copy-done.5), channel_id=1, source_target_pairs={{4,8},{20,24},{8,4},{24,20},{5,9},{21,25},{9,5},{25,21},{6,10},{22... | collective-permute-start | bytes 3145736 | tf_op jit(solution)/shard_map/ppermute | solution.py:258
  29.6 10.5 %copy-start.4 = (s32[32,7]{0,1:T(8,128)S(1)}, s32[32,7]{0,1:T(8,128)}, u32[]{:S(2)}) copy-start(s32[32,7]{0,1:T(8,128)} %param.8) | copy-start | bytes 2692
  29.6 10.7 %collective-permute-start.6 = (bf16[256,1024]{1,0:T(8,128)(2,1)S(1)}, bf16[256,1024]{1,0:T(8,128)(2,1)S(1)}, u32[]{:S(2)}, u32[]{:S(2)}) collective-permute-start(bf16[256,1024]{1,0:T(8,128)(2,1)S(1)} %get-tuple-element.18.top_hbm), channel_id=1, source_target_pairs={{12,16},{16,12},{13,17},{17,13},{14,18},{18,14},{15,19},{19,15}} | collective-permute-start | bytes 1572872 | tf_op jit(solution)/shard_map/ppermute | solution.py:253
  30.3 18.0 %collective-permute-start.8 = (bf16[256,1024]{1,0:T(8,128)(2,1)S(1)}, bf16[256,1024]{1,0:T(8,128)(2,1)S(1)}, u32[]{:S(2)}, u32[]{:S(2)}) collective-permute-start(bf16[256,1024]{1,0:T(8,128)(2,1)S(1)} %collective-permute-done.7), channel_id=1, source_target_pairs={{28,16},{0,12},{29,17},{1,13},{30,18},{2,14},{31,19},{3,15}} | collective-permute-start | bytes 1572872 | tf_op jit(solution)/shard_map/ppermute | solution.py:255
  40.0 31.2 %collective-permute-start.3 = (bf16[4,7,128,128]{3,2,1,0:T(8,128)(2,1)S(1)}, bf16[4,7,128,128]{3,2,1,0:T(8,128)(2,1)S(1)}, u32[]{:S(2)}, u32[]{:S(2)}) collective-permute-start(bf16[4,7,128,128]{3,2,1,0:T(8,128)(2,1)S(1)} %pick.1.f_ref), channel_id=1, source_target_pairs={{4,0},{0,4},{12,8},{8,12},{20,16},{16,20},{28,24},{24,28},{5,1},{1... | collective-permute-start | bytes 2752520 | tf_op jit(solution)/shard_map/ppermute | solution.py:317
  48.3 20.6 %copy-start = (bf16[512,1024]{1,0:T(8,128)(2,1)S(1)}, bf16[512,1024]{1,0:T(8,128)(2,1)}, u32[]{:S(2)}) copy-start(bf16[512,1024]{1,0:T(8,128)(2,1)} %w_ref.3) | copy-start | bytes 3145732
  48.3 20.6 %copy-start.2 = (s32[4,8]{1,0:T(4,128)S(1)}, s32[4,8]{1,0:T(4,128)}, u32[]{:S(2)}) copy-start(s32[4,8]{1,0:T(4,128)} %mask_ref.3) | copy-start | bytes 388
  48.3 20.6 %copy-start.3 = (f32[512]{0:T(512)S(1)}, f32[512]{0:T(512)}, u32[]{:S(2)}) copy-start(f32[512]{0:T(512)} %param.11) | copy-start | bytes 6148
  50.5 15.2 %collective-permute-start.10 = (bf16[512,512]{1,0:T(8,128)(2,1)S(1)}, bf16[512,512]{1,0:T(8,128)(2,1)S(1)}, u32[]{:S(2)}, u32[]{:S(2)}) collective-permute-start(bf16[512,512]{1,0:T(8,128)(2,1)S(1)} %get-tuple-element.14.refs_2_), channel_id=1, source_target_pairs={{1,2},{2,1},{0,0},{3,3},{5,6},{6,5},{4,4},{7,7},{9,10},{10,9},{8,8... | collective-permute-start | bytes 1572872 | tf_op jit(solution)/shard_map/ppermute | solution.py:283
  54.5 14.4 %collective-permute-start.9 = (bf16[512,512]{1,0:T(8,128)(2,1)S(1)}, bf16[512,512]{1,0:T(8,128)(2,1)S(1)}, u32[]{:S(2)}, u32[]{:S(2)}) collective-permute-start(bf16[512,512]{1,0:T(8,128)(2,1)S(1)} %get-tuple-element.13.refs_1_), channel_id=1, source_target_pairs={{0,1},{2,3},{1,0},{3,2},{4,5},{6,7},{5,4},{7,6},{8,9},{10,11},{9,8... | collective-permute-start | bytes 1572872 | tf_op jit(solution)/shard_map/ppermute | solution.py:282
